TPU v7x, 1024 devices: a whole 8x8x8 slice. The times are simulated.
1024 devices in a mesh: seq: 32 (over y_hi, z), res: 32 (over y_lo, x, core).
Axes of the slice: x: 8, y: 8 (y_hi: 4, y_lo: 2; y = y_hi * 2 + y_lo), z: 8, core: 2. Of those that a mesh axis runs over, the one named last changes fastest.
Arguments:
- incoming_homolog_features: bfloat16 [512, 1024, 256], P('seq', 'res'), may hold values from -6 to 6
- alignment_token_index: int32 [512, 1024], P('seq', 'res'), may hold values from 0 to 22
- sequence_mask: int32 [512], replicated, may hold values 0 or 1
- symbol_vector_lookup: bfloat16 [23, 256], replicated, may hold values from -6 to 6
- query_weight: bfloat16 [256, 256], replicated, may hold values from -12 to 12
- lookup_label_matrix: bfloat16 [256, 256], replicated, may hold values from -0.375 to 0.375
- content_matrix: bfloat16 [256, 256], replicated, may hold values from -0.375 to 0.375
- sigmoid_switch_matrix: bfloat16 [256, 256], replicated, may hold values from -0.375 to 0.375
- final_mixing_matrix: bfloat16 [256, 256], replicated, may hold values from -0.375 to 0.375
- first_operand_matrix: bfloat16 [256, 32], replicated, may hold values from -0.375 to 0.375
- second_operand_matrix: bfloat16 [256, 32], replicated, may hold values from -0.375 to 0.375
- pair_weight: bfloat16 [1024, 128], replicated, may hold values from -4 to 4
Outputs:
- revised_homolog_features: bfloat16 [512, 1024, 256], P('seq', 'res')
- pair_output: float32 [1024, 32, 32, 128], P('res', 'seq')
All inputs are finite; a program needn't handle non-finite values.
Results may differ from a plain program's by a relative error of at most 0.012.
The roundings to bfloat16 on the way count: a program that leaves them out, or rounds other values in their place, can miss the bound.
Values may be sent and summed in bfloat16 or wider, within the bound.
A program may use at most 64 MiB of HBM per device.

v0:
```python
import jax
import jax.numpy as jnp
from jax import lax
from jax.sharding import PartitionSpec as P

HEAD_NUMBER = 8
SUBSPACE_SIZE = 32


epsilon = 1e-05


def standardize_features(rows):
    average = jnp.mean(rows, axis=-1, keepdims=True)
    centred = rows - average
    variance = jnp.mean(centred * centred, axis=-1, keepdims=True)
    return centred * lax.rsqrt(variance + epsilon)


def attend(column_block, real_sequence_rows, w_joined, final_mixing_matrix):
    seq_total, piece_count, channel_width = column_block.shape
    standardized_features = standardize_features(column_block.astype(jnp.float32)).astype(
        jnp.bfloat16
    )
    key_bias = (real_sequence_rows - 1.0) * 1000000000.0
    scale_factor = SUBSPACE_SIZE ** (-0.5)
    projected_values = jnp.dot(
        standardized_features.reshape(-1, channel_width),
        w_joined,
        preferred_element_type=jnp.float32,
    ).astype(jnp.bfloat16)
    projected_values = projected_values.reshape(
        seq_total, piece_count, 4, HEAD_NUMBER, SUBSPACE_SIZE
    )
    query_rows = projected_values[:, :, 0]
    key_rows = projected_values[:, :, 1]
    value_rows = projected_values[:, :, 2]
    gate_rows = projected_values[:, :, 3]
    scores = jnp.einsum("sihd,tihd->ihst", query_rows, key_rows, preferred_element_type=jnp.float32)
    scores = scores * scale_factor + key_bias
    softmaxed = jax.nn.softmax(scores, axis=-1).astype(jnp.bfloat16)
    context = jnp.einsum(
        "ihst,tihd->sihd", softmaxed, value_rows, preferred_element_type=jnp.float32
    )
    gated_values = (jax.nn.sigmoid(gate_rows.astype(jnp.float32)) * context).astype(jnp.bfloat16)
    gated_values = gated_values.reshape(-1, HEAD_NUMBER * SUBSPACE_SIZE)
    update = jnp.dot(gated_values, final_mixing_matrix, preferred_element_type=jnp.float32)
    return column_block.astype(jnp.float32) + update.reshape(seq_total, piece_count, channel_width)


def outer_factor_pair(alignment_rows, real_sequence_rows, factor_weight_joined):
    channel_width = alignment_rows.shape[-1]
    standardized_features = standardize_features(alignment_rows.astype(jnp.float32)).astype(
        jnp.bfloat16
    )
    projected_values = jnp.dot(
        standardized_features.reshape(-1, channel_width),
        factor_weight_joined,
        preferred_element_type=jnp.float32,
    )
    projected_values = projected_values.reshape(
        alignment_rows.shape[:-1] + (factor_weight_joined.shape[1],)
    )
    return (projected_values * real_sequence_rows).astype(jnp.bfloat16)


def send_back(updated_state):
    return lax.all_to_all(updated_state[:, None], "seq", split_axis=0, concat_axis=1, tiled=True)


def column_attention_pass(alignment_state, column_update_step):
    return column_update_step(
        lax.all_to_all(alignment_state, "seq", split_axis=1, concat_axis=0, tiled=True)
    )


def per_device(
    incoming_homolog_features,
    alignment_token_index,
    sequence_mask,
    symbol_vector_lookup,
    query_weight,
    lookup_label_matrix,
    content_matrix,
    sigmoid_switch_matrix,
    final_mixing_matrix,
    first_operand_matrix,
    second_operand_matrix,
    pair_weight,
):
    sequence_shards, residue_shards, channel_width = incoming_homolog_features.shape
    sequence_groups = lax.axis_size("seq")
    rows_per_shard = residue_shards // sequence_groups
    seq_total = sequence_mask.shape[0]
    outer_width = first_operand_matrix.shape[1]
    token_class_count = symbol_vector_lookup.shape[0]
    token_indicator = (
        alignment_token_index[:, :, None] == jnp.arange(token_class_count, dtype=jnp.int32)
    ).astype(jnp.bfloat16)
    token_embedding_rows = jnp.dot(
        token_indicator.reshape(-1, token_class_count),
        symbol_vector_lookup,
        preferred_element_type=jnp.float32,
    )
    alignment_state = (
        incoming_homolog_features.astype(jnp.float32).reshape(-1, channel_width)
        + token_embedding_rows
    ).astype(jnp.bfloat16)
    alignment_state = alignment_state.reshape(
        sequence_shards, sequence_groups, rows_per_shard, channel_width
    )
    real_sequence_rows = jnp.maximum(
        sequence_mask, (jnp.arange(seq_total, dtype=jnp.int32) == 0).astype(jnp.int32)
    ).astype(jnp.float32)
    live_count = jnp.sum(real_sequence_rows) + 0.001
    w_joined = jnp.concatenate(
        (query_weight, lookup_label_matrix, content_matrix, sigmoid_switch_matrix), axis=1
    )
    factor_weight_joined = jnp.concatenate((first_operand_matrix, second_operand_matrix), axis=1)

    def column_update_step(column_block):
        updated_state = attend(
            column_block[:, 0], real_sequence_rows, w_joined, final_mixing_matrix
        ).astype(jnp.bfloat16)
        return send_back(updated_state)

    returned_rows = column_attention_pass(alignment_state, column_update_step)
    revised_homolog_features = returned_rows.reshape(sequence_shards, residue_shards, channel_width)
    local_real_rows = lax.dynamic_slice_in_dim(
        real_sequence_rows, lax.axis_index("seq") * sequence_shards, sequence_shards
    )
    outer_factors = outer_factor_pair(
        revised_homolog_features, local_real_rows[:, None, None], factor_weight_joined
    )
    left_panel = lax.all_gather(outer_factors[:, :, :outer_width], "seq", axis=0, tiled=True)
    right_local = outer_factors[:, :, outer_width:].reshape(
        sequence_shards, sequence_groups, rows_per_shard, outer_width
    )
    right_piece = lax.all_to_all(right_local, "seq", split_axis=1, concat_axis=0, tiled=True)
    left_flat = left_panel.reshape(seq_total, residue_shards * outer_width)
    panel_piece = lax.all_gather(right_piece, "res", axis=1, tiled=True)
    group_count = panel_piece.shape[1]
    outer_sum = lax.dot_general(
        left_flat,
        panel_piece.reshape(seq_total, -1),
        (((0,), (0,)), ((), ())),
        preferred_element_type=jnp.float32,
    ).astype(jnp.bfloat16)
    outer_sum = outer_sum.reshape(
        residue_shards, outer_width, group_count, rows_per_shard, outer_width
    )
    outer_sum = outer_sum.transpose(0, 3, 2, 1, 4).reshape(-1, outer_width * outer_width)
    projected_values = (
        jnp.dot(outer_sum, pair_weight, preferred_element_type=jnp.float32) / live_count
    )
    pair_output = projected_values.reshape(
        residue_shards, rows_per_shard, group_count, pair_weight.shape[1]
    )
    return (revised_homolog_features, pair_output)


def solution(mesh):
    return jax.shard_map(
        per_device,
        mesh=mesh,
        in_specs=(
            P("seq", "res", None),
            P("seq", "res"),
            P(),
            P(),
            P(),
            P(),
            P(),
            P(),
            P(),
            P(),
            P(),
            P(),
        ),
        out_specs=(P("seq", "res", None), P("res", "seq", None, None)),
        check_vma=False,
    )
```

profile of v0, /device:TPU:1, one launch (start us, length us, event | category | flops | bytes accessed | tf_op | source)
XLA Modules:
  0.0 294.1 jit_solution(2776165106201849564)
XLA Ops:
  7.2 0.0 copy-start
  7.2 0.8 eq.22
  8.0 1.2 fusion.8
  9.2 0.9 copy.62
  10.1 23.3 %all-to-all-start = ((bf16[16,32,1,256]{3,0,2,1:T(8,128)(2,1)}), bf16[16,32,1,256]{3,0,2,1:T(8,128)(2,1)S(1)}, u32[]{:S(2)}, u32[]{:S(2)}) async-start(bf16[16,32,1,256]{3,0,2,1:T(8,128)(2,1)} %copy.62), calls=%async_computation | async-start | bytes 524288 | tf_op jit(solution)/shard_map/all_to_all | solution.py:73
  33.4 1.3 fusion.37
  34.7 11.2 %all-to-all-done = bf16[16,32,1,256]{3,0,2,1:T(8,128)(2,1)S(1)} async-done(((bf16[16,32,1,256]{3,0,2,1:T(8,128)(2,1)}), bf16[16,32,1,256]{3,0,2,1:T(8,128)(2,1)S(1)}, u32[]{:S(2)}, u32[]{:S(2)}) %all-to-all-start) | async-done | bytes 262176 | tf_op jit(solution)/shard_map/all_to_all | solution.py:73
  45.9 0.1 convert_reduce_fusion.1
  46.1 0.1 div.44
  46.2 0.2 fusion.26
  46.4 0.2 fusion.28
  46.6 1.5 convolution_convert_fusion.1
  48.2 0.5 copy.64
  48.7 5.2 %fusion.38 = (f32[8,512]{1,0:T(8,128)S(1)}, f32[8,512,512]{1,2,0:T(8,128)}) fusion(f32[512]{0:T(512)S(1)} %get-tuple-element.15, bf16[512,1,4,8,32]{0,4,3,2,1:T(8,128)(2,1)S(1)} %bitcast.112), kind=kOutput, calls=%fused_computation.66 | convolution fusion | flops 142606848 | bytes 8931328 | tf_op jit(solution)/shard_map/sub | solution.py:41
  54.0 4.3 %fusion.7 = bf16[512,1,8,32]{0,3,2,1:T(8,128)(2,1)S(1)} fusion(f32[8,512,512]{1,2,0:T(8,128)} %get-tuple-element.17, f32[8,512]{1,0:T(8,128)S(1)} %get-tuple-element.16, bf16[512,1,4,8,32]{0,4,3,2,1:T(8,128)(2,1)S(1)} %bitcast.113), kind=kOutput, calls=%fused_computation.16 | convolution fusion | flops 139198464 | bytes 9191424 | tf_op jit(solution)/shard_map/ihst,tihd->sihd/dot_general | solution.py:42
  58.4 0.3 fusion.12
  58.6 0.5 broadcast.125
  59.1 0.8 reduce.9
  60.0 0.8 reshape.268
  60.7 6.2 %all-to-all-start.1 = ((bf16[32,2,2048]{2,1,0:T(2,128)(2,1)}), bf16[32,2,2048]{2,1,0:T(2,128)(2,1)S(1)}, u32[]{:S(2)}, u32[]{:S(2)}) async-start(bf16[32,2,2048]{2,1,0:T(2,128)(2,1)} %reshape.268), calls=%async_computation.1 | async-start | bytes 524288 | tf_op jit(solution)/shard_map/all_to_all | solution.py:68
  66.9 0.0 all-gather.3.cloned.1.call-start
  67.0 0.1 dynamic_slice.3
  67.1 12.4 %all-to-all-done.1 = bf16[32,2,2048]{2,1,0:T(2,128)(2,1)S(1)} async-done(((bf16[32,2,2048]{2,1,0:T(2,128)(2,1)}), bf16[32,2,2048]{2,1,0:T(2,128)(2,1)S(1)}, u32[]{:S(2)}, u32[]{:S(2)}) %all-to-all-start.1) | async-done | bytes 262176 | tf_op jit(solution)/shard_map/all_to_all | solution.py:68
  79.5 0.3 reshape.269
  79.8 0.1 convert_reduce_fusion
  80.0 0.2 fusion.16
  80.2 0.2 fusion.17
  80.5 0.0 copy-done.3
  80.5 0.0 copy-done.4
  80.5 0.2 fusion.13
  80.7 0.7 slice_bitcast_fusion.14
  81.4 0.0 all-gather.3.cloned.1.call-update
  81.4 0.0 all-gather.5.cloned.1.call-start
  81.5 0.1 copy.87
  81.5 0.1 reshape.270
  81.7 17.1 %all_to_all.42 = bf16[32,2,256]{2,1,0:T(2,128)(2,1)S(1)} all-to-all(bf16[32,2,256]{2,1,0:T(2,128)(2,1)S(1)} %reshape.270), channel_id=1, replica_groups=mesh['seq'=32,'res'=32] {'seq'}, dimensions={0} | all-to-all | bytes 65536 | tf_op jit(solution)/shard_map/all_to_all | solution.py:139
  98.7 0.1 reshape.271
  98.9 0.7 copy.74
  99.6 0.0 all-gather.5.cloned.1.call-update
  100.2 0.8 copy.76
  100.9 83.3 %all-gather.3.cloned.1.call-done = bf16[512,32,32]{2,1,0:T(8,128)(2,1)} async-done(((bf16[16,32,32]{2,1,0:T(8,128)(2,1)}), bf16[512,32,32]{2,1,0:T(8,128)(2,1)}) %all-gather.3.cloned.1.call-update) | async-done | bytes 1048592 | tf_op jit(solution)/shard_map/all_gather | solution.py:135
  184.2 4.4 %copy.72 = bf16[512,32,32]{0,2,1:T(8,128)(2,1)S(1)} copy(bf16[512,32,32]{2,1,0:T(8,128)(2,1)} %all-gather.3.cloned.1.call-done) | data formatting | bytes 2097152 | tf_op jit(solution)/shard_map/all_gather | solution.py:135
  188.7 64.8 %all-gather.5.cloned.1.call-done = bf16[512,32,1,32]{0,3,2,1:T(8,128)(2,1)} async-done(((bf16[512,1,1,32]{0,3,2,1:T(8,128)(2,1)}), bf16[512,32,1,32]{0,3,2,1:T(8,128)(2,1)}) %all-gather.5.cloned.1.call-update) | async-done | bytes 1048592 | tf_op jit(solution)/shard_map/all_gather | solution.py:141
  253.4 2.5 convolution_convert_fusion
  255.9 7.9 %reshape.256 = bf16[32,32,32,1,32]{4,2,1,0,3:T(8,128)(2,1)} reshape(bf16[1024,1024]{1,0:T(8,128)(2,1)S(1)} %convolution_convert_fusion) | data formatting | bytes 4194304 | tf_op jit(solution)/shard_map/reshape | solution.py:149
  263.9 10.5 %copy.86 = bf16[32,32,32,1,32]{4,1,2,0,3:T(8,128)(2,1)} copy(bf16[32,32,32,1,32]{4,2,1,0,3:T(8,128)(2,1)} %reshape.256) | data formatting | bytes 4194304 | tf_op jit(solution)/shard_map/reshape | solution.py:149
  274.4 11.3 %reshape.257 = bf16[1024,1024]{1,0:T(8,128)(2,1)S(1)} reshape(bf16[32,1,32,32,32]{4,3,2,0,1:T(8,128)(2,1)} %bitcast.105) | data formatting | bytes 4194304 | tf_op jit(solution)/shard_map/reshape | solution.py:152
  285.7 1.5 convolution_divide_fusion
  (14 shorter events, 0.1 us)
Async XLA Ops:
  7.2 278.5 %copy-start = (bf16[1024,128]{1,0:T(8,128)(2,1)S(1)}, bf16[1024,128]{1,0:T(8,128)(2,1)}, u32[]{:S(2)}) copy-start(bf16[1024,128]{1,0:T(8,128)(2,1)} %param.23) | copy-start | bytes 786436
  10.1 35.8 %all-to-all-start = ((bf16[16,32,1,256]{3,0,2,1:T(8,128)(2,1)}), bf16[16,32,1,256]{3,0,2,1:T(8,128)(2,1)S(1)}, u32[]{:S(2)}, u32[]{:S(2)}) async-start(bf16[16,32,1,256]{3,0,2,1:T(8,128)(2,1)} %copy.62), calls=%async_computation | async-start | bytes 524288 | tf_op jit(solution)/shard_map/all_to_all | solution.py:73
  54.0 4.4 %copy-start.1 = (bf16[256,256]{1,0:T(8,128)(2,1)S(1)}, bf16[256,256]{1,0:T(8,128)(2,1)}, u32[]{:S(2)}) copy-start(bf16[256,256]{1,0:T(8,128)(2,1)} %param.20) | copy-start | bytes 393220
  54.0 13.0 %copy-start.2 = (s32[512]{0:T(512)S(1)}, s32[512]{0:T(512)}, u32[]{:S(2)}) copy-start(s32[512]{0:T(512)} %param.14) | copy-start | bytes 6148
  54.0 26.5 %copy-start.3 = (bf16[256,32]{0,1:T(8,128)(2,1)S(1)}, bf16[256,32]{0,1:T(8,128)(2,1)}, u32[]{:S(2)}) copy-start(bf16[256,32]{0,1:T(8,128)(2,1)} %param.22) | copy-start | bytes 49156
  54.0 26.5 %copy-start.4 = (bf16[256,32]{0,1:T(8,128)(2,1)S(1)}, bf16[256,32]{0,1:T(8,128)(2,1)}, u32[]{:S(2)}) copy-start(bf16[256,32]{0,1:T(8,128)(2,1)} %param.21) | copy-start | bytes 49156
  60.7 18.8 %all-to-all-start.1 = ((bf16[32,2,2048]{2,1,0:T(2,128)(2,1)}), bf16[32,2,2048]{2,1,0:T(2,128)(2,1)S(1)}, u32[]{:S(2)}, u32[]{:S(2)}) async-start(bf16[32,2,2048]{2,1,0:T(2,128)(2,1)} %reshape.268), calls=%async_computation.1 | async-start | bytes 524288 | tf_op jit(solution)/shard_map/all_to_all | solution.py:68
  66.9 117.3 %all-gather.3.cloned.1.call-start = ((), (), s32[]{:S(2)}) async-start(), calls=%async_computation.3 | async-start | bytes 4325376 | tf_op jit(solution)/shard_map/all_gather | solution.py:135
  81.4 172.0 %all-gather.5.cloned.1.call-start = ((), (), s32[]{:S(2)}) async-start(), calls=%async_computation.4 | async-start | bytes 1081344 | tf_op jit(solution)/shard_map/all_gather | solution.py:141
Sparse Core Ops, SparseCore 0:
  81.5 102.6 all-gather.2
  187.0 66.4 all-gather.4
where the time goes:
time: 295 us; the launch traced here: 294 us
  waiting for transfers between devices  172 us (58%)
  local copies, waits for them, and re-layouts  40.6 us (14%)
  starting transfers between devices  29.6 us (10%)
  blocking collectives  17.1 us (6%)
  matrix products  16.8 us (6%)
  between operations  14.9 us (5%)
  other arithmetic  3.32 us (1%)
    all_gather x1, waiting for transfers between devices, per_device(): lax.all_gather(outer_factors[:, :, :outer_width], 'seq', axis=0, tiled=True)  83.3 us
    all_gather x1, waiting for transfers between devices, per_device(): panel_piece = lax.all_gather(right_piece, 'res', axis=1, tiled=True)  64.8 us
    all_to_all x1, starting transfers between devices, column_attention_pass(): lax.all_to_all(alignment_state, 'seq', split_axis=1, concat_axis=0, tiled...  23.3 us
    reshape x2, local copies, waits for them, and re-layouts, per_device(): outer_sum.reshape(residue_shards, outer_width, group_count, rows_per_shar...  18.4 us
    all_to_all x1, blocking collectives, per_device(): lax.all_to_all(right_local, 'seq', split_axis=1, concat_axis=0, tiled=True)  17.1 us
    all_to_all x1, waiting for transfers between devices, send_back(): lax.all_to_all(updated_state[:, None], 'seq', split_axis=0, concat_axis=1...  12.4 us
    reshape x1, local copies, waits for them, and re-layouts, per_device(): outer_sum.transpose(0, 3, 2, 1, 4).reshape(-1, outer_width * outer_width)  11.3 us
    all_to_all x1, waiting for transfers between devices, column_attention_pass(): lax.all_to_all(alignment_state, 'seq', split_axis=1, concat_axis=0, tiled...  11.2 us
  transfers between devices with their start and end apart: 4, of which 4 were waited for; matrix products, arithmetic and copies ran while one was open for 3% of the time, Pallas kernels for 0%

commit v1 on v0

v1 whole, which is shorter than its diff:
```python
import functools
import math

import jax
import jax.numpy as jnp
from jax import lax
from jax.experimental import pallas as pl
from jax.experimental.pallas import tpu as pltpu
from jax.sharding import PartitionSpec as P

MESH = pl.DeviceIdType.MESH
F32, BF16, I32 = jnp.float32, jnp.bfloat16, jnp.int32
HEADS, SUB, EPS = 8, 32, 1e-5
DIMS = (4, 8, 2, 8)


def standardize(rows):
    centred = rows - jnp.mean(rows, axis=-1, keepdims=True)
    variance = jnp.mean(centred * centred, axis=-1, keepdims=True)
    return centred * lax.rsqrt(variance + EPS)


def dot(a, b):
    return jnp.dot(a, b, preferred_element_type=F32)


def dot_nt(a, b):
    return lax.dot_general(a, b, (((1,), (1,)), ((), ())), preferred_element_type=F32)


def iota(shape, axis):
    return lax.broadcasted_iota(I32, shape, axis)


def one_hot(test):
    return jnp.where(test, 1.0, 0.0).astype(BF16)


def turned(w):
    return w.astype(F32).T.astype(BF16)


def kernel(
    dims, x_ref, tok_ref, mask_ref, table_ref, wq_ref, wk_ref, wv_ref, wg_ref, wo_ref, w1_ref, w2_ref, pw_ref,
    rev_ref, pair_ref,
    snd, col, snd2, back, lt, rt, q_t, k_s, v_t, g_t, ctx, bias, table_s, pw_s, w4, wt, outer, lhs,
    a_send, a_recv, b_send, b_recv, l_send, r_send, y_sem, l_sem, n_sem, r_sem, c_sem,
):
    yh_n, z_n, yl_n, x_n = dims
    ns, nr = yh_n * z_n, yl_n * x_n * 2
    rows = x_ref.shape[0]
    sl = rows // ns
    block = min(256, rows)
    me_s, me_r = lax.axis_index("seq"), lax.axis_index("res")
    yh, z = lax.div(me_s, z_n), lax.rem(me_s, z_n)
    core, x, yl = lax.rem(me_r, 2), lax.rem(lax.div(me_r, 2), x_n), lax.div(me_r, 2 * x_n)

    def res_id(yl_, x_, core_):
        return (yl_ * x_n + x_) * 2 + core_

    def seq_id(b, dz):
        return lax.rem(yh + b, yh_n) * z_n + lax.rem(z + dz + z_n, z_n)

    def res_of(b, dx, core_):
        return res_id(lax.rem(yl + b, yl_n), lax.rem(x + dx + x_n, x_n), core_)

    barrier = pltpu.get_barrier_semaphore()

    def greet(off, carry):
        pl.semaphore_signal(barrier, inc=1, device_id=(lax.rem(me_s + off, ns), me_r), device_id_type=MESH)
        return carry

    lax.fori_loop(1, ns, greet, 0)
    for peer in (res_of(0, 0, 1 - core), res_of(1, 0, core), res_of(0, 1, core), res_of(0, -1, core)):
        pl.semaphore_signal(barrier, inc=1, device_id=(me_s, peer), device_id_type=MESH)

    n_rows = iota((rows, rows), 0)
    sl_bits, ns_bits = sl.bit_length() - 1, ns.bit_length() - 1
    pick = one_hot(iota((rows, rows), 1) == (n_rows & (sl - 1)) * ns + (n_rows >> sl_bits))
    n_seq = iota((rows, sl), 0) & (sl - 1)
    token_rows = dot(one_hot(iota((rows, sl), 1) == n_seq), tok_ref[...].astype(F32).astype(BF16))
    own = (iota((rows, ns), 0) >> sl_bits) == iota((rows, ns), 1)
    token = jnp.sum(jnp.where(own, token_rows, 0.0), axis=1, keepdims=True)
    kinds = table_ref.shape[0]
    table_s[...] = jnp.zeros_like(table_s)
    table_s[0:kinds, :] = table_ref[...].astype(F32)
    classes = table_s.shape[0]
    token_hot = one_hot(iota((rows, classes), 1).astype(F32) == token)
    msa = (dot(pick, x_ref[...]) + dot(token_hot, table_s[...].astype(BF16))).astype(BF16)
    snd[...] = msa.reshape(snd.shape)
    col[pl.ds(me_s, 1)] = snd[pl.ds(me_s, 1)]

    pl.semaphore_wait(barrier, ns - 1 + 4)

    def send_out(off, carry):
        to = lax.rem(me_s + off, ns)
        pltpu.make_async_remote_copy(
            src_ref=snd.at[to], dst_ref=col.at[me_s], send_sem=a_send, recv_sem=a_recv,
            device_id=(to, me_r), device_id_type=MESH,
        ).start()
        return carry

    lax.fori_loop(1, ns, send_out, 0)

    wt[0:256, :] = turned(wq_ref[...])
    wt[256:512, :] = turned(wv_ref[...])
    wt[512:768, :] = turned(wg_ref[...])
    wt[768:800, :] = turned(w1_ref[...])
    wt[800:832, :] = turned(w2_ref[...])
    live = jnp.where(iota((1, rows), 1) == 0, 1, mask_ref[...]).astype(F32)
    live_col = jnp.sum(jnp.where(n_rows == iota((rows, rows), 1), live, 0.0), axis=1, keepdims=True)
    bias[...] = jnp.broadcast_to((live_col - 1.0) * 1e9, bias.shape)
    count = jnp.sum(live, axis=1, keepdims=True) + 0.001
    pw_s[...] = pw_ref[...].astype(F32)
    w4[...] = jnp.zeros_like(w4)

    def spread(e, carry):
        part = pw_s[pl.ds(e, 32, stride=32), :].astype(BF16)
        for i in range(4):
            w4[pl.ds(pl.multiple_of(e * 128 + i * 32, 32), 32), i * 128 : (i + 1) * 128] = part
        return carry

    lax.fori_loop(0, 32, spread, 0)

    pltpu.make_async_copy(snd.at[pl.ds(0, ns - 1)], col.at[pl.ds(0, ns - 1)], a_recv).wait()

    column = col[...].reshape(rows, 256).astype(F32)
    normed = standardize(column).astype(BF16)
    k_s[...] = dot(normed, wk_ref[...]).astype(BF16)
    q_t[...] = dot_nt(wt[0:256, :], normed).astype(BF16).astype(F32)
    v_t[...] = dot_nt(wt[256:512, :], normed).astype(BF16)
    g_t[...] = jax.nn.sigmoid(dot_nt(wt[512:768, :], normed).astype(BF16).astype(F32))
    factor = SUB**-0.5 * math.log2(math.e)

    def head(h, carry):
        at = pl.multiple_of(lax.div(h, 4) * 128, 128)
        here = pl.multiple_of(h * SUB, SUB)
        keys = k_s[:, pl.ds(at, 128)]
        query = jnp.where((iota((128, rows), 0) >> 5) == lax.rem(h, 4), q_t[pl.ds(at, 128), :], 0.0).astype(BF16)
        values = v_t[pl.ds(here, SUB), :]
        for b in range(rows // block):
            part = slice(b * block, (b + 1) * block)
            scores = dot(keys, query[:, part]) + bias[...]
            top = jnp.max(scores, axis=0, keepdims=True)
            weights = jnp.exp2((scores - top) * factor)
            total = jnp.sum(weights, axis=0, keepdims=True)
            ctx[pl.ds(here, SUB), part] = dot(values, weights.astype(BF16)) / total
        return carry

    lax.fori_loop(0, HEADS, head, 0)
    gated = (g_t[...] * ctx[...]).T.astype(BF16)
    revised = (column + dot(gated, wo_ref[...])).astype(BF16)
    snd2[...] = revised.reshape(snd2.shape)
    back[pl.ds(me_s, 1)] = snd2[pl.ds(me_s, 1)]
    normed = standardize(revised.astype(F32)).astype(BF16)
    factors = (dot_nt(wt[768:832, :], normed) * live).astype(BF16)
    lt[pl.ds(me_s, 1)] = factors[0:32].reshape(1, 32, rows)
    rt[pl.ds(me_r, 1)] = factors[32:64].reshape(1, 32, rows)

    def part_of(buf, at, half):
        return buf.at[at] if half is None else buf.at[at, pl.ds(16 * half, 16)]

    def push(buf, at, dev, send, recv, half=None):
        ref = part_of(buf, at, half)
        pltpu.make_async_remote_copy(
            src_ref=ref, dst_ref=ref, send_sem=send, recv_sem=recv, device_id=dev, device_id_type=MESH
        ).start()

    def arrived(buf, at, recv, half=None):
        ref = part_of(buf, at, half)
        pltpu.make_async_copy(ref, ref, recv).wait()

    def ring(buf, n, index, device, send, sems):
        far = n // 2

        def give(b, way, k):
            step = 1 - 2 * way
            half = way if k + 1 == far else None
            push(buf, index(b, -step * k), device(step), send, sems.at[(b * 2 + way) * far + k], half)

        def take(b, way, k):
            step = 1 - 2 * way
            half = way if k == far else None
            arrived(buf, index(b, -step * k), sems.at[(b * 2 + way) * far + k - 1], half)

        return far, give, take

    l_far, l_give, l_take = ring(lt, z_n, seq_id, lambda s: (seq_id(0, s), me_r), l_send, l_sem)
    r_far, r_give, r_take = ring(
        rt, x_n, lambda b, d: res_of(b, d, core), lambda s: (me_s, res_of(0, s, core)), r_send, r_sem
    )
    mate = (me_s, res_of(0, 0, 1 - core))

    def hand_over(b, dx):
        push(rt, res_of(b, dx, core), mate, r_send, c_sem.at[b * x_n + dx % x_n])

    for way in range(2):
        l_give(0, way, 0)
        r_give(0, way, 0)
    push(rt, me_r, (me_s, res_of(1, 0, core)), r_send, n_sem)
    for b in range(1, yh_n):
        push(lt, me_s, (seq_id(b, 0), me_r), l_send, y_sem.at[yh_n - b - 1])
    hand_over(0, 0)

    def send_back(off, carry):
        to = lax.rem(me_s + off, ns)
        pltpu.make_async_remote_copy(
            src_ref=snd2.at[to], dst_ref=back.at[me_s], send_sem=b_send, recv_sem=b_recv,
            device_id=(to, me_r), device_id_type=MESH,
        ).start()
        return carry

    lax.fori_loop(1, ns, send_back, 0)

    def r_step(k):
        for b in range(2):
            for way in range(2):
                r_take(b, way, k)
                if k < r_far:
                    r_give(b, way, k)
                    hand_over(b, k * (2 * way - 1))
            if k == r_far:
                hand_over(b, k)

    def l_step(k):
        for b in range(yh_n):
            for way in range(2):
                l_take(b, way, k)
                if k < l_far:
                    l_give(b, way, k)

    arrived(rt, res_of(1, 0, core), n_sem)
    for way in range(2):
        r_give(1, way, 0)
    hand_over(1, 0)
    for b in range(1, yh_n):
        arrived(lt, seq_id(b, 0), y_sem.at[b - 1])
        for way in range(2):
            l_give(b, way, 0)
    for k in range(1, max(r_far, l_far) + 1):
        if k <= r_far:
            r_step(k)
        if k <= l_far:
            l_step(k)
    for b in range(2):
        for dx in range(x_n):
            arrived(rt, res_of(b, dx, 1 - core), c_sem.at[b * x_n + dx])

    right = rt[...].reshape(nr * 32, rows)
    wide = min(256, ns * 32)
    tiles = wide // 128

    def outer_part(n, carry):
        left = lt[pl.ds(n * (wide // 32), wide // 32)].reshape(wide, rows)
        product = dot_nt(right, left)
        for t in range(tiles):
            outer[n * tiles + t] = product[:, t * 128 : (t + 1) * 128]
        return carry

    lax.fori_loop(0, ns * 32 // wide, outer_part, 0)

    def gather_part(e, carry):
        at = pl.multiple_of(e * 128, 128)
        for g in range(ns // 4):
            part = outer[g, pl.ds(e, nr, stride=32), :]
            lhs[g * nr : (g + 1) * nr, pl.ds(at, 128)] = part.astype(BF16)
        return carry

    lax.fori_loop(0, 32, gather_part, 0)
    pair = dot(lhs[...], w4[...]) / count
    for g in range(ns // 4):
        for i in range(4):
            pair_ref[4 * g + i] = pair[g * nr : (g + 1) * nr, i * 128 : (i + 1) * 128]

    pltpu.make_async_copy(snd2.at[pl.ds(0, ns - 1)], back.at[pl.ds(0, ns - 1)], b_recv).wait()
    unpick = one_hot(iota((rows, rows), 1) == (n_rows & (ns - 1)) * sl + (n_rows >> ns_bits))
    rev_ref[...] = dot(unpick, back[...].reshape(rows, 256)).astype(BF16)

    pltpu.make_async_copy(snd.at[pl.ds(0, ns - 1)], snd.at[pl.ds(0, ns - 1)], a_send).wait()
    pltpu.make_async_copy(snd2.at[pl.ds(0, ns - 1)], snd2.at[pl.ds(0, ns - 1)], b_send).wait()
    pltpu.make_async_copy(lt.at[pl.ds(0, ns - 1)], lt.at[pl.ds(0, ns - 1)], l_send).wait()
    pltpu.make_async_copy(rt.at[pl.ds(0, nr - 1)], rt.at[pl.ds(0, nr - 1)], r_send).wait()


def per_device(dims, features, tokens, mask, table, wq, wk, wv, wg, wo, w1, w2, pw):
    yh_n, z_n, yl_n, x_n = dims
    ns, nr = yh_n * z_n, yl_n * x_n * 2
    sl, res_local, width = features.shape
    rows = sl * res_local
    block = min(256, rows)
    vmem = pl.BlockSpec(memory_space=pltpu.VMEM)
    dma = pltpu.SemaphoreType.DMA
    revised, pair = pl.pallas_call(
        functools.partial(kernel, dims),
        out_shape=(
            jax.ShapeDtypeStruct((rows, width), BF16),
            jax.ShapeDtypeStruct((ns, nr, pw.shape[1]), F32),
        ),
        in_specs=[vmem] * 12,
        out_specs=(vmem, vmem),
        scratch_shapes=[
            pltpu.VMEM((ns, sl, width), BF16),
            pltpu.VMEM((ns, sl, width), BF16),
            pltpu.VMEM((ns, sl, width), BF16),
            pltpu.VMEM((ns, sl, width), BF16),
            pltpu.VMEM((ns, 32, rows), BF16),
            pltpu.VMEM((nr, 32, rows), BF16),
            pltpu.VMEM((256, rows), F32),
            pltpu.VMEM((rows, 256), BF16),
            pltpu.VMEM((256, rows), BF16),
            pltpu.VMEM((256, rows), F32),
            pltpu.VMEM((256, rows), F32),
            pltpu.VMEM((rows, block), F32),
            pltpu.VMEM((32, width), F32),
            pltpu.VMEM(pw.shape, F32),
            pltpu.VMEM((32 * 128, 512), BF16),
            pltpu.VMEM((832, 256), BF16),
            pltpu.VMEM((ns // 4, nr * 32, 128), F32),
            pltpu.VMEM((ns // 4 * nr, 32 * 128), BF16),
            dma, dma, dma, dma, dma, dma,
            dma((yh_n - 1,)),
            dma((yh_n * z_n,)),
            dma,
            dma((yl_n * x_n,)),
            dma((yl_n * x_n,)),
        ],
        compiler_params=pltpu.CompilerParams(collective_id=0, has_side_effects=True),
    )(
        features.reshape(rows, width), tokens, mask.reshape(1, -1), table,
        wq, wk, wv, wg, wo, w1, w2, pw,
    )
    return revised.reshape(features.shape), pair.reshape(ns, 1, nr, pw.shape[1])


def solution(mesh, dims=DIMS):
    return jax.shard_map(
        functools.partial(per_device, dims),
        mesh=mesh,
        in_specs=(P("seq", "res", None), P("seq", "res")) + (P(),) * 10,
        out_specs=(P("seq", "res", None), P("res", "seq", None, None)),
        check_vma=False,
    )
```

time: 295 us -> 81.1 us (0.27)
  waiting for transfers between devices: 172 us -> 0 us
  Pallas kernels: 0 us -> 75.5 us
  local copies, waits for them, and re-layouts: 40.6 us -> 4.72 us
  starting transfers between devices: 29.6 us -> 0 us
  blocking collectives: 17.1 us -> 0 us
  matrix products: 16.8 us -> 0 us
  between operations: 14.9 us -> 0.66 us
  other arithmetic: 3.32 us -> 0 us
    all_gather x2 -> x0, waiting for transfers between devices: 148 us -> none  [the longest x1 83.3 us: per_device(): lax.all_gather(outer_factors[:, :, :outer_width], 'seq', axis=0, tiled=True)]
    pallas_call x0 -> x1, Pallas kernels: none -> 75.5 us  [per_device(): pl.pallas_call(functools.partial(kernel, dims), out_shape=(jax.ShapeDtype...]
    reshape x6 -> x0, local copies, waits for them, and re-layouts: 31.4 us -> none  [the longest x2 18.4 us: per_device(): outer_sum.reshape(residue_shards, outer_width, group_count, rows_per_shar...]
    all_to_all x2 -> x0, starting transfers between devices: 29.5 us -> none  [the longest x1 23.3 us: column_attention_pass(): lax.all_to_all(alignment_state, 'seq', split_axis=1, concat_axis=0, tiled...]
    all_to_all x2 -> x0, waiting for transfers between devices: 23.7 us -> none  [the longest x1 12.4 us: send_back(): lax.all_to_all(updated_state[:, None], 'seq', split_axis=0, concat_axis=1...]
    all_to_all x1 -> x0, blocking collectives: 17.1 us -> none  [per_device(): lax.all_to_all(right_local, 'seq', split_axis=1, concat_axis=0, tiled=True)]
    dot_general x7 -> x0, matrix products: 11.6 us -> none  [the longest x1 4.29 us: attend(): jnp.einsum('ihst,tihd->sihd', softmaxed, value_rows, preferred_element_ty...]
    sub x1 -> x0, matrix products: 5.23 us -> none  [attend(): softmaxed = jax.nn.softmax(scores, axis=-1).astype(jnp.bfloat16)]
  transfers between devices with their start and end apart: 4 -> 0, of which waited for: 4 -> 0; matrix products, arithmetic and copies ran while one was open for 3% -> 0% of each run, Pallas kernels for 0% -> 0%
where the time goes in v1:
time: 81.1 us; the launch traced here: 80.9 us
  Pallas kernels  75.5 us (93%)
  local copies, waits for them, and re-layouts  4.72 us (6%)
    pallas_call x1, Pallas kernels, per_device(): pl.pallas_call(functools.partial(kernel, dims), out_shape=(jax.ShapeDtype...  75.5 us
    unnamed x8, local copies, waits for them, and re-layouts  4.72 us

profile of v1, /device:TPU:1, one launch (start us, length us, event | category | flops | bytes accessed | tf_op | source)
XLA Modules:
  0.0 80.9 jit_solution(11098333659165399608)
XLA Ops:
  0.6 0.0 copy-start.1
  0.6 1.5 %copy.14.w1_ref = bf16[256,32]{1,0:T(8,128)(2,1)} copy(bf16[256,32]{0,1:T(8,128)(2,1)} %param.21) | data formatting | bytes 32768 | tf_op args[9]
  2.1 0.0 copy-done.1
  2.1 0.7 copy.15.w2_ref
  2.8 75.5 %shard_map.131 = (bf16[512,256]{1,0:T(8,128)(2,1)}, f32[32,32,128]{2,1,0:T(8,128)}) custom-call(bf16[512,256]{1,0:T(8,128)(2,1)} %bitcast.8, s32[16,32]{1,0:T(8,128)} %tok_ref.1, s32[1,512]{1,0:T(1,128)} %bitcast.9, bf16[23,256]{1,0:T(8,128)(2,1)} %table_ref.1, bf16[256,256]{1,0:T(8,128)(2,1)} %wq_ref.1, bf16[256,256]{1,0:T(8,128)(2,1)} %wk_ref.1, ...), custom_call_target="tpu_custom_call" | custom-call | tf_op jit(solution)/shard_map/pallas_call | solution.py:293
  78.3 0.0 copy-start
  78.4 1.7 %copy.19 = bf16[16,32,256]{2,1,0:T(8,128)(2,1)} copy(bf16[16,32,256]{2,1,0:T(8,128)(2,1)} %bitcast.7) | data formatting | bytes 524288
  80.1 0.0 copy-done
  80.1 0.8 copy.20
Async XLA Ops:
  0.6 1.5 %copy-start.1 = (bf16[256,32]{0,1:T(8,128)(2,1)S(1)}, bf16[256,32]{0,1:T(8,128)(2,1)}, u32[]{:S(2)}) copy-start(bf16[256,32]{0,1:T(8,128)(2,1)} %param.22) | copy-start | bytes 49156
  78.3 1.7 %copy-start = (f32[32,32,128]{2,1,0:T(8,128)S(1)}, f32[32,32,128]{2,1,0:T(8,128)}, u32[]{:S(2)}) copy-start(f32[32,32,128]{2,1,0:T(8,128)} %get-tuple-element.5) | copy-start | bytes 1572868

commit v2 on v1

v2 whole, which is shorter than its diff:
```python
import functools
import math

import jax
import jax.numpy as jnp
from jax import lax
from jax.experimental import pallas as pl
from jax.experimental.pallas import tpu as pltpu
from jax.sharding import PartitionSpec as P

MESH = pl.DeviceIdType.MESH
F32, BF16, I32 = jnp.float32, jnp.bfloat16, jnp.int32
HEADS, SUB, EPS = 8, 32, 1e-5
DIMS = (4, 8, 2, 8)
VMEM_BYTES = 36 << 20
SCHEDULE = (
    "r", "s", "c", "L01", "R01", "N", "B2", "Y1", "Y3", "Y2", "B2", "L02", "R02", "R11",
    "L11", "L31", "L21", "B4", "L03", "R03", "R12", "L12", "L32", "L22", "B4", "R04", "R13", "L13",
    "L33", "L23", "B4", "R14", "P", "O1", "O2", "O3", "L04", "L14", "L34", "L24", "O4",
)


def standardize(rows):
    centred = rows - jnp.mean(rows, axis=-1, keepdims=True)
    variance = jnp.mean(centred * centred, axis=-1, keepdims=True)
    return centred * lax.rsqrt(variance + EPS)


def dot(a, b):
    return jnp.dot(a, b, preferred_element_type=F32)


def dot_nt(a, b):
    return lax.dot_general(a, b, (((1,), (1,)), ((), ())), preferred_element_type=F32)


def iota(shape, axis):
    return lax.broadcasted_iota(I32, shape, axis)


def one_hot(test):
    return jnp.where(test, 1.0, 0.0).astype(BF16)


def turned(w):
    return w.astype(F32).T.astype(BF16)


def kernel(
    dims, x_h, tok_h, mask_h, table_h, wq_h, wk_h, wv_h, wg_h, wo_h, w1_h, w2_h, pw_h,
    rev_ref, pair_ref,
    x_ref, tok_ref, mask_ref, table_ref, wq_ref, wk_ref, wv_ref, wg_ref, wo_ref, pw_ref,
    snd, col, snd2, back, lt, rt, q_t, k_s, v_t, g_t, ctx, bias, table_s, pw_s, w4, wt, perm, rp, fac, lhs,
    in_sem, a_send, a_recv, b_send, b_recv, l_send, r_send, y_sem, l_sem, n_sem, r_sem, c_sem,
):
    yh_n, z_n, yl_n, x_n = dims
    ns, nr = yh_n * z_n, yl_n * x_n * 2
    half_n, zh_n = ns // 2, z_n // 2
    rows = x_ref.shape[0]
    sl = rows // ns
    block = rows // 2
    me_s, me_r = lax.axis_index("seq"), lax.axis_index("res")
    yh, z = lax.div(me_s, z_n), lax.rem(me_s, z_n)
    core, x, yl = lax.rem(me_r, 2), lax.rem(lax.div(me_r, 2), x_n), lax.div(me_r, 2 * x_n)
    zh = lax.div(z, 2)
    slot = lax.rem(z, 2) * half_n + yh * zh_n + zh

    def seq_id(b, dz):
        return lax.rem(yh + b, yh_n) * z_n + lax.rem(z + dz + z_n, z_n)

    def left_at(b, dz):
        return lax.rem(z + dz + z_n, z_n) * yh_n + lax.rem(yh + b, yh_n)

    def res_of(b, dx, core_):
        return (lax.rem(yl + b, yl_n) * x_n + lax.rem(x + dx + x_n, x_n)) * 2 + core_

    loads = [
        pltpu.make_async_copy(src, dst, in_sem.at[i])
        for i, (src, dst) in enumerate((
            (tok_h, tok_ref), (table_h, table_ref), (x_h, x_ref), (mask_h, mask_ref), (wq_h, wq_ref), (wk_h, wk_ref), (wv_h, wv_ref), (wg_h, wg_ref), (wo_h, wo_ref),
            (w1_h, wt.at[pl.ds(768, 32)]), (w2_h, wt.at[pl.ds(800, 32)]), (pw_h, pw_ref),
        ))
    ]
    for load in loads[:3]:
        load.start()

    barrier = pltpu.get_barrier_semaphore()

    def greet(off, carry):
        pl.semaphore_signal(barrier, inc=1, device_id=(lax.rem(me_s + off, ns), me_r), device_id_type=MESH)
        return carry

    lax.fori_loop(1, ns, greet, 0)
    for peer in (res_of(0, 0, 1 - core), res_of(1, 0, core), res_of(0, 1, core), res_of(0, -1, core)):
        pl.semaphore_signal(barrier, inc=1, device_id=(me_s, peer), device_id_type=MESH)
    for load in loads[3:]:
        load.start()

    n_rows = iota((rows, rows), 0)
    n_cols = iota((rows, rows), 1)
    sl_bits, ns_bits = sl.bit_length() - 1, ns.bit_length() - 1
    pick = one_hot(n_cols == (n_rows & (sl - 1)) * ns + (n_rows >> sl_bits))
    loads[0].wait()
    loads[1].wait()
    n_seq = iota((rows, sl), 0) & (sl - 1)
    token_rows = dot(one_hot(iota((rows, sl), 1) == n_seq), tok_ref[...].astype(F32).astype(BF16))
    own = (iota((rows, ns), 0) >> sl_bits) == iota((rows, ns), 1)
    token = jnp.sum(jnp.where(own, token_rows, 0.0), axis=1, keepdims=True)
    kinds = table_ref.shape[0]
    table_s[...] = jnp.zeros_like(table_s)
    table_s[0:kinds, :] = table_ref[...].astype(F32)
    classes = table_s.shape[0]
    token_hot = one_hot(iota((rows, classes), 1).astype(F32) == token)
    embedded = dot(token_hot, table_s[...].astype(BF16))
    loads[2].wait()
    msa = (dot(pick, x_ref[...]) + embedded).astype(BF16)
    snd[...] = msa.reshape(snd.shape)
    col[pl.ds(slot, 1)] = snd[pl.ds(me_s, 1)]

    pl.semaphore_wait(barrier, ns - 1 + 4)

    def send_out(t, carry):
        off = lax.rem(t * 11, ns)
        to = lax.rem(yh + lax.div(off, z_n), yh_n) * z_n + lax.rem(z + lax.rem(off, z_n), z_n)
        pltpu.make_async_remote_copy(
            src_ref=snd.at[to], dst_ref=col.at[slot], send_sem=a_send, recv_sem=a_recv,
            device_id=(to, me_r), device_id_type=MESH,
        ).start()
        return carry

    lax.fori_loop(1, ns, send_out, 0)

    for load in loads[3:]:
        load.wait()
    wt[0:256, :] = turned(wq_ref[...])
    wt[256:512, :] = turned(wv_ref[...])
    wt[512:768, :] = turned(wg_ref[...])
    live_all = jnp.where(iota((16, rows), 1) == 0, 1, mask_ref[...]).astype(F32)
    count = jnp.sum(live_all[0:1], axis=1, keepdims=True) + 0.001
    place = n_cols >> sl_bits
    spot = place & (half_n - 1)
    zh_bits = zh_n.bit_length() - 1
    device = (spot >> zh_bits) * z_n + (spot & (zh_n - 1)) * 2 + jnp.where(place >= half_n, 1, 0)
    order = one_hot(n_rows == device * sl + (n_cols & (sl - 1)))
    live = dot(live_all.astype(BF16), order)[0:1]
    live_col = jnp.sum(jnp.where(n_rows == n_cols, live, 0.0), axis=1, keepdims=True)
    bias[...] = jnp.broadcast_to((live_col - 1.0) * 1e9, bias.shape)
    wide = nr * 32
    turn = iota((256, 256), 0)
    perm[...] = one_hot(iota((256, 256), 1) == (turn & 7) * 32 + (turn >> 3))
    pw_s[...] = pw_ref[...].astype(F32)
    w4[...] = jnp.zeros_like(w4)

    def spread(e, carry):
        part = pw_s[pl.ds(e, 32, stride=32), :].astype(BF16)
        for i in range(4):
            w4[pl.ds(pl.multiple_of(e * 128 + i * 32, 32), 32), i * 128 : (i + 1) * 128] = part
        return carry

    lax.fori_loop(0, 32, spread, 0)

    pltpu.make_async_copy(snd.at[pl.ds(0, ns - 1)], col.at[pl.ds(0, ns - 1)], a_recv).wait()

    normed = standardize(col[...].reshape(rows, 256).astype(F32)).astype(BF16)
    k_s[...] = dot(normed, wk_ref[...]).astype(BF16)
    q_t[...] = dot_nt(wt[0:256, :], normed).astype(BF16).astype(F32)
    v_t[...] = dot_nt(wt[256:512, :], normed).astype(BF16)
    g_t[...] = jax.nn.sigmoid(dot_nt(wt[512:768, :], normed).astype(BF16).astype(F32))
    factor = SUB**-0.5 * math.log2(math.e)

    def one_head(h, part):
        at = pl.multiple_of(lax.div(h, 4) * 128, 128)
        here = pl.multiple_of(h * SUB, SUB)
        query = jnp.where((iota((128, block), 0) >> 5) == lax.rem(h, 4), q_t[pl.ds(at, 128), part], 0.0).astype(BF16)
        scores = dot(k_s[:, pl.ds(at, 128)], query) + bias[...]
        top = jnp.max(scores, axis=0, keepdims=True)
        weights = jnp.exp2((scores - top) * factor)
        total = jnp.sum(weights, axis=0, keepdims=True)
        ctx[pl.ds(here, SUB), part] = dot(v_t[pl.ds(here, SUB), :], weights.astype(BF16)) / total

    def attend(b):
        part = slice(b * block, (b + 1) * block)

        def heads(h, carry):
            for j in range(2):
                one_head(h * 2 + j, part)
            return carry

        lax.fori_loop(0, HEADS // 2, heads, 0)
        gated = (g_t[:, part] * ctx[:, part]).T.astype(BF16)
        column = col[b * half_n : (b + 1) * half_n].reshape(block, 256).astype(F32)
        revised = (column + dot(gated, wo_ref[...])).astype(BF16)
        snd2[b * half_n : (b + 1) * half_n] = revised.reshape(half_n, sl, 256)
        again = standardize(revised.astype(F32)).astype(BF16)
        fac[:, part] = (dot_nt(wt[768:832, :], again) * live[:, part]).astype(BF16)

    def send_back(b, first, last):
        def one(t, carry):
            off = lax.rem(t * 5, half_n)
            to_y = lax.rem(yh + lax.div(off, zh_n), yh_n)
            to_z = lax.rem(zh + lax.rem(off, zh_n), zh_n)
            to = to_y * z_n + to_z * 2 + b

            @pl.when(to != me_s)
            def _():
                pltpu.make_async_remote_copy(
                    src_ref=snd2.at[b * half_n + to_y * zh_n + to_z], dst_ref=back.at[me_s],
                    send_sem=b_send, recv_sem=b_recv, device_id=(to, me_r), device_id_type=MESH,
                ).start()

            return carry

        lax.fori_loop(first, last, one, 0)

    def part_of(buf, at, half):
        return buf.at[at] if half is None else buf.at[at, pl.ds(16 * half, 16)]

    def push(buf, at, dev, send, recv, half=None):
        ref = part_of(buf, at, half)
        pltpu.make_async_remote_copy(
            src_ref=ref, dst_ref=ref, send_sem=send, recv_sem=recv, device_id=dev, device_id_type=MESH
        ).start()

    def arrived(buf, at, recv, half=None):
        ref = part_of(buf, at, half)
        pltpu.make_async_copy(ref, ref, recv).wait()

    def ring(buf, n, index, device, send, sems):
        far = n // 2

        def give(b, way, k):
            step = 1 - 2 * way
            half = way if k + 1 == far else None
            push(buf, index(b, -step * k), device(step), send, sems.at[(b * 2 + way) * far + k], half)

        def take(b, way, k):
            step = 1 - 2 * way
            half = way if k == far else None
            arrived(buf, index(b, -step * k), sems.at[(b * 2 + way) * far + k - 1], half)

        return far, give, take

    l_far, l_give, l_take = ring(lt, z_n, left_at, lambda s: (seq_id(0, s), me_r), l_send, l_sem)
    r_far, r_give, r_take = ring(
        rt, x_n, lambda b, d: res_of(b, d, core), lambda s: (me_s, res_of(0, s, core)), r_send, r_sem
    )
    mate = (me_s, res_of(0, 0, 1 - core))

    def hand_over(b, dx):
        push(rt, res_of(b, dx, core), mate, r_send, c_sem.at[b * x_n + dx % x_n])

    def r_step(k):
        for b in range(2):
            for way in range(2):
                r_take(b, way, k)
                if k < r_far:
                    r_give(b, way, k)
                    hand_over(b, k * (2 * way - 1))
            if k == r_far:
                hand_over(b, k)

    def l_step(k):
        for b in range(yh_n):
            for way in range(2):
                l_take(b, way, k)
                if k < l_far:
                    l_give(b, way, k)

    attend(0)
    send_back(0, 0, half_n)
    attend(1)
    lt[pl.ds(left_at(0, 0), 1)] = fac[0:32, :].reshape(1, 32, rows)
    rt[pl.ds(me_r, 1)] = fac[32:64, :].reshape(1, 32, rows)
    back[pl.ds(me_s, 1)] = snd2[pl.ds(slot, 1)]

    def start_row():
        push(rt, me_r, (me_s, res_of(1, 0, core)), r_send, n_sem)

    def start_rings():
        for way in range(2):
            l_give(0, way, 0)
            r_give(0, way, 0)

    def start_columns():
        for b in range(1, yh_n):
            push(lt, left_at(0, 0), (seq_id(b, 0), me_r), l_send, y_sem.at[yh_n - b - 1])

    def next_row():
        arrived(rt, res_of(1, 0, core), n_sem)
        for way in range(2):
            r_give(1, way, 0)
        hand_over(1, 0)

    def next_column(b):
        arrived(lt, left_at(b, 0), y_sem.at[b - 1])
        for way in range(2):
            l_give(b, way, 0)

    def r_step(b, k):
        if 1 <= k <= r_far:
            for way in range(2):
                r_take(b, way, k)
                if k < r_far:
                    r_give(b, way, k)
                    hand_over(b, k * (2 * way - 1))
            if k == r_far:
                hand_over(b, k)

    def l_step(b, k):
        if 1 <= k <= l_far:
            for way in range(2):
                l_take(b, way, k)
                if k < l_far:
                    l_give(b, way, k)

    def right_rows():
        for b in range(2):
            for dx in range(x_n):
                arrived(rt, res_of(b, dx, 1 - core), c_sem.at[b * x_n + dx])
        for n in range(nr // 8):
            eight = rt[n * 8 : (n + 1) * 8].reshape(256, rows)
            rp[n * 256 : (n + 1) * 256, :] = dot(perm[...], eight).astype(BF16)

    groups = []

    def outer_part(*distances):
        lefts = []
        for dz in distances:
            group = lax.rem(z + dz + z_n, z_n)
            groups.append(group)
            lefts.append(lt[pl.ds(group * yh_n, yh_n)].reshape(yh_n * 32, rows))
        product = dot_nt(rp[...], jnp.concatenate(lefts, axis=0))
        for j in range(len(distances)):
            to = (len(groups) - len(distances) + j) * nr
            for e in range(32):
                lane = slice(j * 128, (j + 1) * 128)
                eights = [product[n * 256 + e * 8 : n * 256 + (e + 1) * 8, lane] for n in range(nr // 8)]
                lhs[to : to + nr, e * 128 : (e + 1) * 128] = jnp.concatenate(eights, axis=0).astype(BF16)

    sent = 0
    for word in SCHEDULE:
        kind, args = word[0], [int(c) for c in word[1:]]
        if kind == "r":
            start_row()
            hand_over(0, 0)
        elif kind == "s":
            start_rings()
        elif kind == "c":
            start_columns()
        elif kind == "N":
            next_row()
        elif kind == "Y":
            next_column(*args)
        elif kind == "R":
            r_step(*args)
        elif kind == "L":
            l_step(*args)
        elif kind == "P":
            right_rows()
        elif kind == "B":
            more = min(args[0], half_n - sent)
            send_back(1, sent, sent + more)
            sent += more
        elif kind == "O":
            if args[0] < l_far:
                outer_part(-args[0], args[0])
            elif args[0] == l_far:
                outer_part(0, l_far)

    pair = dot(lhs[...], w4[...]) / count
    for n, group in enumerate(groups):
        for i in range(4):
            pair_ref[i * z_n + group] = pair[n * nr : (n + 1) * nr, i * 128 : (i + 1) * 128]

    pltpu.make_async_copy(snd2.at[pl.ds(0, ns - 1)], back.at[pl.ds(0, ns - 1)], b_recv).wait()
    unpick = one_hot(n_cols == (n_rows & (ns - 1)) * sl + (n_rows >> ns_bits))
    rev_ref[...] = dot(unpick, back[...].reshape(rows, 256)).astype(BF16)

    pltpu.make_async_copy(snd.at[pl.ds(0, ns - 1)], snd.at[pl.ds(0, ns - 1)], a_send).wait()
    pltpu.make_async_copy(snd2.at[pl.ds(0, ns - 1)], snd2.at[pl.ds(0, ns - 1)], b_send).wait()
    pltpu.make_async_copy(lt.at[pl.ds(0, ns - 1)], lt.at[pl.ds(0, ns - 1)], l_send).wait()
    pltpu.make_async_copy(rt.at[pl.ds(0, nr - 1)], rt.at[pl.ds(0, nr - 1)], r_send).wait()


def per_device(dims, features, tokens, mask, table, wq, wk, wv, wg, wo, w1, w2, pw):
    yh_n, z_n, yl_n, x_n = dims
    ns, nr = yh_n * z_n, yl_n * x_n * 2
    sl, res_local, width = features.shape
    rows = sl * res_local
    vmem, hbm = pl.BlockSpec(memory_space=pltpu.VMEM), pl.BlockSpec(memory_space=pltpu.HBM)
    dma = pltpu.SemaphoreType.DMA
    revised, pair = pl.pallas_call(
        functools.partial(kernel, dims),
        out_shape=(
            jax.ShapeDtypeStruct((rows, width), BF16),
            jax.ShapeDtypeStruct((ns, nr, pw.shape[1]), F32),
        ),
        in_specs=[hbm] * 12,
        out_specs=(vmem, vmem),
        scratch_shapes=[
            pltpu.VMEM((rows, width), BF16),
            pltpu.VMEM(tokens.shape, I32),
            pltpu.VMEM((1, rows), I32),
            pltpu.VMEM(table.shape, BF16),
            *[pltpu.VMEM((width, width), BF16)] * 5,
            pltpu.VMEM(pw.shape, BF16),
            *[pltpu.VMEM((ns, sl, width), BF16)] * 4,
            pltpu.VMEM((ns, 32, rows), BF16),
            pltpu.VMEM((nr, 32, rows), BF16),
            pltpu.VMEM((256, rows), F32),
            pltpu.VMEM((rows, 256), BF16),
            pltpu.VMEM((256, rows), BF16),
            pltpu.VMEM((256, rows), F32),
            pltpu.VMEM((256, rows), F32),
            pltpu.VMEM((rows, rows // 2), F32),
            pltpu.VMEM((32, width), F32),
            pltpu.VMEM(pw.shape, F32),
            pltpu.VMEM((32 * 128, 512), BF16),
            pltpu.VMEM((832, 256), BF16),
            pltpu.VMEM((256, 256), BF16),
            pltpu.VMEM((nr * 32, rows), BF16),
            pltpu.VMEM((64, rows), BF16),
            pltpu.VMEM((z_n * nr, 32 * 128), BF16),
            dma((12,)),
            dma, dma, dma, dma, dma, dma,
            dma((yh_n - 1,)),
            dma((yh_n * z_n,)),
            dma,
            dma((yl_n * x_n,)),
            dma((yl_n * x_n,)),
        ],
        compiler_params=pltpu.CompilerParams(
            collective_id=0, has_side_effects=True, vmem_limit_bytes=VMEM_BYTES
        ),
    )(
        *[
            pltpu.with_memory_space_constraint(a, pltpu.HBM)
            for a in (
                features.reshape(rows, width), tokens, mask.reshape(1, -1), table,
                wq, wk, wv, wg, wo, w1.T, w2.T, pw,
            )
        ]
    )
    return revised.reshape(features.shape), pair.reshape(ns, 1, nr, pw.shape[1])


def solution(mesh, dims=DIMS):
    return jax.shard_map(
        functools.partial(per_device, dims),
        mesh=mesh,
        in_specs=(P("seq", "res", None), P("seq", "res")) + (P(),) * 10,
        out_specs=(P("seq", "res", None), P("res", "seq", None, None)),
        check_vma=False,
    )
```

time: 81.1 us -> 70.6 us (0.87)
  Pallas kernels: 75.5 us -> 68.3 us
  local copies, waits for them, and re-layouts: 4.72 us -> 1.5 us
    pallas_call x1, Pallas kernels: 75.5 us -> 68.3 us  [per_device(): pl.pallas_call(functools.partial(kernel, dims), out_shape=(jax.ShapeDtype...]
    unnamed x8 -> x2, local copies, waits for them, and re-layouts: 4.72 us -> 1.5 us
where the time goes in v2:
time: 70.6 us; the launch traced here: 70.4 us
  Pallas kernels  68.3 us (97%)
  local copies, waits for them, and re-layouts  1.5 us (2%)
    pallas_call x1, Pallas kernels, per_device(): pl.pallas_call(functools.partial(kernel, dims), out_shape=(jax.ShapeDtype...  68.3 us
    unnamed x2, local copies, waits for them, and re-layouts  1.5 us

profile of v2, /device:TPU:1, one launch (start us, length us, event | category | flops | bytes accessed | tf_op | source)
XLA Modules:
  0.0 70.4 jit_solution(3580027246481521693)
XLA Ops:
  0.6 68.3 %shard_map.131 = (bf16[512,256]{1,0:T(8,128)(2,1)S(1)}, f32[32,32,128]{2,1,0:T(8,128)S(1)}) custom-call(bf16[512,256]{1,0:T(8,128)(2,1)} %bitcast.10, s32[16,32]{1,0:T(8,128)} %tok_h.1, s32[1,512]{1,0:T(1,128)} %bitcast.13, bf16[23,256]{1,0:T(8,128)(2,1)} %table_h.1, bf16[256,256]{1,0:T(8,128)(2,1)} %wq_h.1, bf16[256,256]{1,0:T(8,128)(2,1)} %wk_h.1, ...), custom_call_target="tpu_custom_call" | custom-call | tf_op jit(solution)/shard_map/pallas_call | solution.py:392
  68.9 0.7 %copy.17 = bf16[16,32,256]{2,1,0:T(8,128)(2,1)} copy(bf16[16,32,256]{2,1,0:T(8,128)(2,1)S(1)} %bitcast.9) | data formatting | bytes 524288
  69.6 0.8 %copy.18 = f32[32,1,32,128]{3,2,1,0:T(8,128)} copy(f32[32,1,32,128]{3,2,1,0:T(8,128)S(1)} %bitcast.8) | data formatting | bytes 1048576

commit v3 on v2

--- a/solution.py
+++ b/solution.py
@@ -168,11 +168,13 @@
     g_t[...] = jax.nn.sigmoid(dot_nt(wt[512:768, :], normed).astype(BF16).astype(F32))
     factor = SUB**-0.5 * math.log2(math.e)
 
-    def one_head(h, part):
+    def scores_of(h, part):
         at = pl.multiple_of(lax.div(h, 4) * 128, 128)
+        query = jnp.where((iota((128, block), 0) >> 5) == lax.rem(h, 4), q_t[pl.ds(at, 128), part], 0.0).astype(BF16)
+        return dot(k_s[:, pl.ds(at, 128)], query) + bias[...]
+
+    def weigh(h, part, scores):
         here = pl.multiple_of(h * SUB, SUB)
-        query = jnp.where((iota((128, block), 0) >> 5) == lax.rem(h, 4), q_t[pl.ds(at, 128), part], 0.0).astype(BF16)
-        scores = dot(k_s[:, pl.ds(at, 128)], query) + bias[...]
         top = jnp.max(scores, axis=0, keepdims=True)
         weights = jnp.exp2((scores - top) * factor)
         total = jnp.sum(weights, axis=0, keepdims=True)
@@ -182,11 +184,13 @@
         part = slice(b * block, (b + 1) * block)
 
         def heads(h, carry):
-            for j in range(2):
-                one_head(h * 2 + j, part)
+            ahead = scores_of(h * 4, part)
+            for j in range(4):
+                scores, ahead = ahead, scores_of(h * 4 + j + 1, part) if j < 3 else None
+                weigh(h * 4 + j, part, scores)
             return carry
 
-        lax.fori_loop(0, HEADS // 2, heads, 0)
+        lax.fori_loop(0, HEADS // 4, heads, 0)
         gated = (g_t[:, part] * ctx[:, part]).T.astype(BF16)
         column = col[b * half_n : (b + 1) * half_n].reshape(block, 256).astype(F32)
         revised = (column + dot(gated, wo_ref[...])).astype(BF16)

time: 70.6 us -> 68.4 us (0.969)
  Pallas kernels: 68.3 us -> 66.1 us
    pallas_call x1, Pallas kernels: 68.3 us -> 66.1 us  [per_device(): pl.pallas_call(functools.partial(kernel, dims), out_shape=(jax.ShapeDtype...]
where the time goes in v3:
time: 68.4 us; the launch traced here: 68.3 us
  Pallas kernels  66.1 us (97%)
  local copies, waits for them, and re-layouts  1.5 us (2%)
    pallas_call x1, Pallas kernels, per_device(): pl.pallas_call(functools.partial(kernel, dims), out_shape=(jax.ShapeDtype...  66.1 us
    unnamed x2, local copies, waits for them, and re-layouts  1.5 us

profile of v3, /device:TPU:1, one launch (start us, length us, event | category | flops | bytes accessed | tf_op | source)
XLA Modules:
  0.0 68.3 jit_solution(4398521256715898763)
XLA Ops:
  0.6 66.1 %shard_map.131 = (bf16[512,256]{1,0:T(8,128)(2,1)S(1)}, f32[32,32,128]{2,1,0:T(8,128)S(1)}) custom-call(bf16[512,256]{1,0:T(8,128)(2,1)} %bitcast.10, s32[16,32]{1,0:T(8,128)} %tok_h.1, s32[1,512]{1,0:T(1,128)} %bitcast.13, bf16[23,256]{1,0:T(8,128)(2,1)} %table_h.1, bf16[256,256]{1,0:T(8,128)(2,1)} %wq_h.1, bf16[256,256]{1,0:T(8,128)(2,1)} %wk_h.1, ...), custom_call_target="tpu_custom_call" | custom-call | tf_op jit(solution)/shard_map/pallas_call | solution.py:396
  66.8 0.7 %copy.17 = bf16[16,32,256]{2,1,0:T(8,128)(2,1)} copy(bf16[16,32,256]{2,1,0:T(8,128)(2,1)S(1)} %bitcast.9) | data formatting | bytes 524288
  67.5 0.8 %copy.18 = f32[32,1,32,128]{3,2,1,0:T(8,128)} copy(f32[32,1,32,128]{3,2,1,0:T(8,128)S(1)} %bitcast.8) | data formatting | bytes 1048576
